TPU v7x, 32 devices: a whole 2x2x4 slice. The times are simulated.
32 devices in a mesh: grp: 2 (over x), wide: 4 (over y, core), head: 4 (over z).
Axes of the slice: x: 2, y: 2, z: 4, core: 2. Of those that a mesh axis runs over, the one named last changes fastest.
Arguments:
- tokens: bfloat16 [64, 8192], P('grp'), parts along dimension 0, may hold values from -30 to 30
- attn_gain: bfloat16 [8192], replicated, may hold values from 0.25 to 1.75
- ffn_gain: bfloat16 [8192], P('wide'), may hold values from 0.25 to 1.75
- w_query: bfloat16 [8192, 8192], P('wide', 'head'), may hold values from -0.0625 to 0.0625
- key_matrix: bfloat16 [8192, 1024], P('wide', 'head'), may hold values from -0.0625 to 0.0625
- value_matrix: bfloat16 [8192, 1024], P('wide', 'head'), may hold values from -0.0625 to 0.0625
- w_out: bfloat16 [8192, 8192], P('head', 'wide'), may hold values from -0.0625 to 0.0625
- w_gate: bfloat16 [8192, 14336], P('wide', 'head'), may hold values from -0.0625 to 0.0625
- w_up: bfloat16 [8192, 14336], P('wide', 'head'), may hold values from -0.0625 to 0.0625
- w_down: bfloat16 [14336, 8192], P('head', 'wide'), may hold values from -0.046875 to 0.046875
- kv_cache: bfloat16 [2, 16, 2048, 1024], P(None, 'grp', 'wide', 'head'), parts along dimension 1, may hold values from -250 to 250
- lengths: int32 [16], P('grp'), parts along dimension 0, may hold values from 1 to 2048, 8192 in all
- slots: int32 [16], P('grp'), parts along dimension 0, may hold values from 0 to 7, each once
Outputs:
- layer_out: bfloat16 [64, 8192], P(('grp', 'head'), 'wide'), parts along dimension 0
There are 2 independent parts, one for each index of `grp`. A program takes and returns all parts, laid end to end along the dimension named above; an argument that names none is the same for every part. Nothing has to cross between parts.
Inputs may be any that keep to these rules, and one draw needn't show every extreme that they name: `lengths`: they sum to 8192, and the longest is exactly 2048. `slots`: each slot belongs to exactly one request.
All inputs are finite; a program needn't handle non-finite values.
Results may differ from a plain program's by a relative error of at most 0.0057.
Values may be sent and summed in bfloat16 or wider, within the bound.
A program may use at most 128 MiB of HBM per device.

v0:
```python
import jax
import jax.numpy as jnp
from jax import lax
from jax.sharding import PartitionSpec as P

MODEL_WIDTH = 8192
HEAD_WIDTH = 128
DRAFT_TOKENS = 4


epsilon = 1e-05
theta_base = 500000.0
neg_large = -1e30


def rotary_tables(values, token_positions):
    half_width = values.shape[-1] // 2
    exponent = jnp.arange(half_width, dtype=jnp.float32) * (2.0 / values.shape[-1])
    angles = token_positions[:, None] * (theta_base ** (-exponent))[None, :]
    cosine = jnp.cos(angles)[:, None, :]
    sine_part = jnp.sin(angles)[:, None, :]
    front_half = values[..., :half_width]
    back_half = values[..., half_width:]
    return jnp.concatenate(
        [front_half * cosine - back_half * sine_part, back_half * cosine + front_half * sine_part],
        axis=-1,
    )


def finish(query_sum, key_total, value_total, token_positions):
    row_count = query_sum.shape[0]
    rotated_queries = rotary_tables(
        query_sum.reshape(row_count, -1, HEAD_WIDTH), token_positions
    ) * HEAD_WIDTH ** (-0.5)
    rotated_keys = rotary_tables(key_total.reshape(row_count, -1, HEAD_WIDTH), token_positions)
    return (
        rotated_queries.reshape(row_count, -1).astype(jnp.bfloat16),
        rotated_keys.reshape(row_count, -1).astype(jnp.bfloat16),
        value_total.astype(jnp.bfloat16),
    )


def per_device(
    tokens,
    attn_gain,
    ffn_gain,
    w_query,
    key_matrix,
    value_matrix,
    w_out,
    w_gate,
    w_up,
    w_down,
    kv_cache,
    lengths,
    slots,
):
    token_row_count = tokens.shape[0]
    col_width = w_query.shape[0]
    head_size = lax.axis_size("head")
    wide_at = lax.axis_index("wide")
    head_at = lax.axis_index("head")
    tokens_f = tokens.astype(jnp.float32)
    scale_in = lax.rsqrt(jnp.mean(tokens_f * tokens_f, axis=1, keepdims=True) + epsilon)
    normed = (tokens_f * scale_in * attn_gain.astype(jnp.float32)[None, :]).astype(jnp.bfloat16)
    own_cols = lax.dynamic_slice_in_dim(normed, wide_at * col_width, col_width, 1)
    query_part = jnp.dot(own_cols, w_query, preferred_element_type=jnp.float32)
    key_part = jnp.dot(own_cols, key_matrix, preferred_element_type=jnp.float32)
    value_part = jnp.dot(own_cols, value_matrix, preferred_element_type=jnp.float32)
    token_positions = (
        jnp.repeat(lengths, DRAFT_TOKENS)
        + jnp.arange(token_row_count, dtype=jnp.int32) % DRAFT_TOKENS
    ).astype(jnp.float32)
    query_sum, key_total, value_total = lax.psum((query_part, key_part, value_part), "wide")
    query_all, key_new, fresh_value = finish(query_sum, key_total, value_total, token_positions)
    requests = lengths.shape[0]
    kv_local = key_matrix.shape[1] // HEAD_WIDTH
    heads_per_group = w_query.shape[1] // HEAD_WIDTH // kv_local
    ctx_local = kv_cache.shape[2]
    ordered = jnp.take(kv_cache, slots, axis=1)
    keys_local = ordered[0].reshape(requests, ctx_local, kv_local, HEAD_WIDTH)
    vals_local = ordered[1].reshape(requests, ctx_local, kv_local, HEAD_WIDTH)
    query_blocks = query_all.reshape(requests, DRAFT_TOKENS, kv_local, heads_per_group, HEAD_WIDTH)
    scores = jnp.einsum(
        "rjkgd,rpkd->rkgjp", query_blocks, keys_local, preferred_element_type=jnp.float32
    )
    live_mask = (wide_at * ctx_local + jnp.arange(ctx_local, dtype=jnp.int32))[None, :] < lengths[
        :, None
    ]
    live_full = live_mask[:, None, None, None, :]
    masked = jnp.where(live_full, scores, neg_large)
    local_top = jnp.max(masked, axis=-1)
    draft_keys = key_new.reshape(requests, DRAFT_TOKENS, kv_local, HEAD_WIDTH)
    draft_vals = fresh_value.reshape(requests, DRAFT_TOKENS, kv_local, HEAD_WIDTH)
    draft_scores = jnp.einsum(
        "rjkgd,rikd->rkgji", query_blocks, draft_keys, preferred_element_type=jnp.float32
    )
    causal = (
        jnp.arange(DRAFT_TOKENS, dtype=jnp.int32)[None, :]
        <= jnp.arange(DRAFT_TOKENS, dtype=jnp.int32)[:, None]
    )
    draft_masked = jnp.where(causal, draft_scores, neg_large)
    cache_top = lax.pmax(local_top, "wide")
    top_all = jnp.maximum(cache_top, jnp.max(draft_masked, axis=-1))
    weights = jnp.where(live_full, jnp.exp(masked - top_all[..., None]), 0.0)
    partial_acc = jnp.einsum(
        "rkgjp,rpkd->rkgjd",
        weights.astype(jnp.bfloat16),
        vals_local,
        preferred_element_type=jnp.float32,
    )
    cache_total, cache_acc = lax.psum((jnp.sum(weights, axis=-1), partial_acc), "wide")
    draft_weights = jnp.where(causal, jnp.exp(draft_masked - top_all[..., None]), 0.0)
    denominator = cache_total + jnp.sum(draft_weights, axis=-1)
    draft_acc = jnp.einsum(
        "rkgji,rikd->rkgjd",
        draft_weights.astype(jnp.bfloat16),
        draft_vals,
        preferred_element_type=jnp.float32,
    )
    attended = (
        ((cache_acc + draft_acc) / denominator[..., None])
        .transpose(0, 3, 1, 2, 4)
        .reshape(token_row_count, -1)
        .astype(jnp.bfloat16)
    )
    out_part = jnp.dot(attended, w_out, preferred_element_type=jnp.float32)
    own_tokens = lax.dynamic_slice_in_dim(tokens_f, wide_at * col_width, col_width, 1)
    gain_f = ffn_gain.astype(jnp.float32)[None, :]
    share_head = token_row_count // head_size
    attn_share = lax.psum_scatter(out_part, "head", scatter_dimension=0, tiled=True)
    token_rows = lax.dynamic_slice_in_dim(own_tokens, head_at * share_head, share_head, 0)
    resid_rows = (token_rows + attn_share).astype(jnp.bfloat16)
    resid_f = resid_rows.astype(jnp.float32)
    square_sum = lax.psum(jnp.sum(resid_f * resid_f, axis=1), "wide")
    normed_share = (
        resid_f * lax.rsqrt(square_sum / MODEL_WIDTH + epsilon)[:, None] * gain_f
    ).astype(jnp.bfloat16)
    ffn_in = lax.all_gather(normed_share, "head", axis=0, tiled=True)
    gate_part = jnp.dot(ffn_in, w_gate, preferred_element_type=jnp.float32)
    up_part = jnp.dot(ffn_in, w_up, preferred_element_type=jnp.float32)
    gate_sum, up_sum = lax.psum((gate_part, up_part), "wide")
    hidden = (jax.nn.silu(gate_sum) * up_sum).astype(jnp.bfloat16)
    ffn_out = lax.psum_scatter(
        jnp.dot(hidden, w_down, preferred_element_type=jnp.float32),
        "head",
        scatter_dimension=0,
        tiled=True,
    )
    return (resid_rows.astype(jnp.float32) + ffn_out).astype(jnp.bfloat16)


def solution(mesh):
    in_specs = (
        P("grp", None),
        P(),
        P("wide"),
        P("wide", "head"),
        P("wide", "head"),
        P("wide", "head"),
        P("head", "wide"),
        P("wide", "head"),
        P("wide", "head"),
        P("head", "wide"),
        P(None, "grp", "wide", "head"),
        P("grp"),
        P("grp"),
    )
    out_specs = P(("grp", "head"), "wide")
    return jax.shard_map(
        per_device, mesh=mesh, in_specs=in_specs, out_specs=out_specs, check_vma=False
    )
```

profile of v0, /device:TPU:0, one launch (start us, length us, event | category | flops | bytes accessed | tf_op | source)
XLA Modules:
  0.0 235.9 jit_solution(7514440644843655939)
XLA Ops:
  6.5 1.2 convert_element_type.65
  7.8 1.6 multiply_reduce_fusion
  9.4 0.7 dynamic-slice
  10.1 5.0 %convolution_bitcast_fusion = f32[4,8,16,128]{3,1,2,0:T(8,128)S(1)} fusion(bf16[2048,2048]{1,0:T(8,128)(2,1)} %param.16, f32[32,8192]{1,0:T(8,128)S(1)} %convert_element_type.65, s32[]{:T(128)S(6)} %select_n.50, f32[2048]{0:T(1024)S(1)} %dynamic-slice, f32[32]{0:T(128)S(1)} %add_rsqrt_fusion.1), kind=kOutput, calls=%fused_computation.4 | convolution fusion | flops 268632064 | bytes 8921604 | tf_op jit(solution)/shard_map/dot_general | solution.py:67
  15.1 0.8 copy.46
  16.0 4.9 %gather_fusion = bf16[8,2,512,256]{3,2,1,0:T(8,128)(2,1)} fusion(bf16[2,8,512,256]{3,2,1,0:T(8,128)(2,1)} %param.23, s32[1024]{0:T(1024)S(1)} %pad_clamp_fusion), kind=kCustom, calls=%fused_computation | custom fusion | bytes 8388640 | tf_op jit(solution)/shard_map/jit(_take)/gather | solution.py:80
  20.9 2.7 %select_bitcast_fusion = bf16[2,8,512,256]{3,2,0,1:T(8,128)(2,1)S(1)} fusion(bf16[8,2,512,256]{3,2,1,0:T(8,128)(2,1)} %gather_fusion, pred[8]{0:T(512)(128)(4,1)S(1)} %compare_and_fusion), kind=kLoop, calls=%fused_computation.1 | loop fusion | flops 2097152 | bytes 8388616 | tf_op jit(solution)/shard_map/jit(_take)/select_n | solution.py:80
  23.6 2.3 fusion.36
  26.5 13.0 %psum.57 = f32[32,2,128]{2,0,1:T(8,128)S(1)} all-reduce(f32[32,2,128]{2,0,1:T(8,128)S(1)} %bitcast.52), channel_id=1, replica_groups=mesh['grp'=2,'wide'=4,'head'=4] {'wide'}, use_global_device_ids=true, to_apply=%region_4.5 | all-reduce | flops 8192 | bytes 65536 | tf_op jit(solution)/shard_map/psum | solution.py:74
  40.1 2.9 %copy.29 = bf16[1,8,512,256]{2,3,1,0:T(8,128)(2,1)S(1)} copy(bf16[1,8,512,256]{3,2,0,1:T(8,128)(2,1)} %get-tuple-element.12) | data formatting | bytes 4194304 | tf_op jit(solution)/shard_map/slice | solution.py:82
  42.9 3.9 %copy.23 = bf16[1,8,512,256]{2,3,1,0:T(8,128)(2,1)} copy(bf16[1,8,512,256]{3,2,0,1:T(8,128)(2,1)} %get-tuple-element.11) | data formatting | bytes 4194304 | tf_op jit(solution)/shard_map/slice | solution.py:81
  47.0 4.1 %all-reduce.6.cloned.1.call-done = f32[32,16,128]{2,1,0:T(8,128)} async-done(((f32[32,16,128]{2,1,0:T(8,128)}), f32[32,16,128]{2,1,0:T(8,128)}) %all-reduce.6.cloned.1.call-update) | async-done | bytes 262160 | tf_op jit(solution)/shard_map/psum | solution.py:74
  51.0 1.2 multiply_subtract_fusion
  52.4 2.1 fusion.37
  54.5 10.3 %pmax.7 = f32[8,2,8,4]{2,3,1,0:T(4,128)S(1)} all-reduce(f32[8,2,8,4]{2,3,1,0:T(4,128)S(1)} %get-tuple-element.19), channel_id=1, replica_groups=mesh['grp'=2,'wide'=4,'head'=4] {'wide'}, use_global_device_ids=true, to_apply=%region_3.4 | all-reduce | flops 512 | bytes 4096 | tf_op jit(solution)/shard_map/pmax | solution.py:103
  64.8 0.7 fusion.38
  65.5 1.5 fusion.7
  67.1 0.4 fusion.5
  67.5 10.8 %all-reduce = (f32[8,2,8,4]{2,3,1,0:T(4,128)S(1)}, bf16[32,256]{1,0:T(8,128)(2,1)S(1)}) all-reduce(f32[8,2,8,4]{2,3,1,0:T(4,128)S(1)} %fusion.5, f32[32,256]{1,0:T(8,128)S(1)} %fusion.41), channel_id=1, replica_groups=mesh['grp'=2,'wide'=4,'head'=4] {'wide'}, use_global_device_ids=true, to_apply=%region_9.10 | all-reduce | flops 8704 | bytes 53248 | tf_op jit(solution)/shard_map/psum | solution.py:112
  78.5 21.1 %all-reduce.8.cloned.1.call-done = f32[8,2,8,4,128]{4,2,3,1,0:T(8,128)} async-done(((f32[8,2,8,4,128]{4,2,3,1,0:T(8,128)}), f32[8,2,8,4,128]{4,2,3,1,0:T(8,128)}) %all-reduce.8.cloned.1.call-update) | async-done | bytes 262160 | tf_op jit(solution)/shard_map/psum | solution.py:112
  99.6 1.3 fusion.3
  101.0 5.6 %fusion.43 = f32[32,2048]{1,0:T(8,128)} fusion(bf16[32,2048]{1,0:T(8,128)(2,1)S(1)} %convert_element_type.77, bf16[2048,2048]{1,0:T(8,128)(2,1)} %param.19), kind=kOutput, calls=%fused_computation.73 | convolution fusion | flops 268435456 | bytes 8781824 | tf_op jit(solution)/shard_map/dot_general | solution.py:127
  106.7 20.1 %reduce-scatter.3.cloned.1.call-done = f32[8,2048]{1,0:T(8,128)} async-done(((f32[32,2048]{1,0:T(8,128)}), f32[8,2048]{1,0:T(8,128)}) %reduce-scatter.3.cloned.1.call-update) | async-done | bytes 65552 | tf_op jit(solution)/shard_map/reduce_scatter | solution.py:131
  126.8 1.1 fusion.22
  128.0 5.7 %psum.61 = f32[8]{0:T(128)S(1)} all-reduce(f32[8]{0:T(128)S(1)} %get-tuple-element.9), channel_id=1, replica_groups=mesh['grp'=2,'wide'=4,'head'=4] {'wide'}, use_global_device_ids=true, to_apply=%region_13.14 | all-reduce | flops 8 | bytes 64 | tf_op jit(solution)/shard_map/psum | solution.py:135
  133.7 13.6 %all_gather.3 = bf16[32,2048]{1,0:T(8,128)(2,1)S(1)} all-gather(bf16[8,2048]{1,0:T(8,128)(2,1)S(1)} %fusion.24), channel_id=1, replica_groups=mesh['grp'=2,'wide'=4,'head'=4] {'head'}, dimensions={0}, use_global_device_ids=true | all-gather | bytes 163840 | tf_op jit(solution)/shard_map/all_gather | solution.py:139
  147.3 8.5 %fusion.45 = f32[32,3584]{1,0:T(8,128)} fusion(bf16[32,2048]{1,0:T(8,128)(2,1)S(1)} %all_gather.3, bf16[2048,3584]{1,0:T(8,128)(2,1)} %param.21), kind=kOutput, calls=%fused_computation.75 | convolution fusion | flops 469762048 | bytes 15269888 | tf_op jit(solution)/shard_map/dot_general | solution.py:141
  155.8 8.5 %fusion.44 = f32[32,3584]{1,0:T(8,128)} fusion(bf16[32,2048]{1,0:T(8,128)(2,1)S(1)} %all_gather.3, bf16[2048,3584]{1,0:T(8,128)(2,1)} %param.20), kind=kOutput, calls=%fused_computation.74 | convolution fusion | flops 469762048 | bytes 15269888 | tf_op jit(solution)/shard_map/dot_general | solution.py:140
  164.5 34.0 %all-reduce.10.cloned.1.call-done = (f32[32,3584]{1,0:T(8,128)}, f32[32,3584]{1,0:T(8,128)}) async-done(((f32[32,3584]{1,0:T(8,128)}, f32[32,3584]{1,0:T(8,128)}), (f32[32,3584]{1,0:T(8,128)}, f32[32,3584]{1,0:T(8,128)})) %all-reduce.10.cloned.1.call-update) | async-done | bytes 917520 | tf_op jit(solution)/shard_map/psum | solution.py:142
  198.5 8.9 %fusion.15 = f32[32,2048]{1,0:T(8,128)} fusion(bf16[3584,2048]{1,0:T(8,128)(2,1)} %param.22, f32[32,3584]{1,0:T(8,128)} %get-tuple-element.7, f32[32,3584]{1,0:T(8,128)} %get-tuple-element.8), kind=kOutput, calls=%fused_computation.28 | convolution fusion | flops 470450176 | bytes 15859712 | tf_op jit(solution)/shard_map/dot_general | solution.py:145
  207.4 20.5 %reduce-scatter.5.cloned.1.call-done = f32[8,2048]{1,0:T(8,128)} async-done(((f32[32,2048]{1,0:T(8,128)}), f32[8,2048]{1,0:T(8,128)}) %reduce-scatter.5.cloned.1.call-update) | async-done | bytes 65552 | tf_op jit(solution)/shard_map/reduce_scatter | solution.py:144
  227.9 1.5 fusion.25
  (51 shorter events, 2.1 us)
Async XLA Ops:
  6.5 19.6 %copy-start = (bf16[2048,256]{1,0:T(8,128)(2,1)S(1)}, bf16[2048,256]{1,0:T(8,128)(2,1)}, u32[]{:S(2)}) copy-start(bf16[2048,256]{1,0:T(8,128)(2,1)} %param.17) | copy-start | bytes 3145732
  6.5 44.5 %all-reduce.6.cloned.1.call-start = ((), (), s32[]{:S(2)}) async-start(), calls=%async_computation.2 | async-start | bytes 524288 | tf_op jit(solution)/shard_map/psum | solution.py:74
  7.7 31.7 %copy-start.2 = (f32[32,8192]{1,0:T(8,128)}, f32[32,8192]{1,0:T(8,128)S(1)}, u32[]{:S(2)}) copy-start(f32[32,8192]{1,0:T(8,128)S(1)} %convert_element_type.65) | copy-start | bytes 3145732
  10.1 5.8 %copy-start.6 = (s32[8]{0:T(128)S(1)}, s32[8]{0:T(128)}, u32[]{:S(2)}) copy-start(s32[8]{0:T(128)} %param.25) | copy-start | bytes 100
  15.9 83.7 %all-reduce.8.cloned.1.call-start = ((), (), s32[]{:S(2)}) async-start(), calls=%async_computation.3 | async-start | bytes 524288 | tf_op jit(solution)/shard_map/psum | solution.py:112
  23.6 2.3 copy-start.5
  23.6 15.9 %copy-start.3 = (bf16[2048,256]{1,0:T(8,128)(2,1)S(1)}, bf16[2048,256]{1,0:T(8,128)(2,1)}, u32[]{:S(2)}) copy-start(bf16[2048,256]{1,0:T(8,128)(2,1)} %param.18) | copy-start | bytes 3145732
  67.0 59.8 %reduce-scatter.3.cloned.1.call-start = ((), (), s32[]{:S(2)}) async-start(), calls=%async_computation.4 | async-start | bytes 327680 | tf_op jit(solution)/shard_map/reduce_scatter | solution.py:131
  101.0 5.7 %copy-start.4 = (bf16[2048]{0:T(1024)(128)(2,1)S(1)}, bf16[2048]{0:T(1024)(128)(2,1)}, u32[]{:S(2)}) copy-start(bf16[2048]{0:T(1024)(128)(2,1)} %param.15) | copy-start | bytes 12292
  106.6 91.9 %all-reduce.10.cloned.1.call-start = ((), (), s32[]{:S(2)}) async-start(), calls=%async_computation.6 | async-start | bytes 1835008 | tf_op jit(solution)/shard_map/psum | solution.py:142
  164.4 63.5 %reduce-scatter.5.cloned.1.call-start = ((), (), s32[]{:S(2)}) async-start(), calls=%async_computation.5 | async-start | bytes 327680 | tf_op jit(solution)/shard_map/reduce_scatter | solution.py:144
  198.5 30.8 %copy-start.1 = (bf16[2048,256]{1,0:T(8,128)(2,1)S(1)}, bf16[2048,256]{1,0:T(8,128)(2,1)}, u32[]{:S(2)}) copy-start(bf16[2048,256]{1,0:T(8,128)(2,1)} %param.17) | copy-start | bytes 3145732
Sparse Core Ops, SparseCore 0:
  16.0 34.9 all-reduce.5
  67.2 32.4 all-reduce.7
  106.8 19.9 reduce-scatter.2
  164.5 33.9 all-reduce.9
  207.5 20.3 reduce-scatter.4
where the time goes:
time: 237 us; the launch traced here: 236 us
  waiting for transfers between devices  99.8 us (42%)
  blocking collectives  53.3 us (22%)
  matrix products  42.7 us (18%)
  local copies, waits for them, and re-layouts  15.8 us (7%)
  between operations  13.4 us (6%)
  other arithmetic  10.5 us (4%)
    psum x1, waiting for transfers between devices, per_device(): gate_sum, up_sum = lax.psum((gate_part, up_part), 'wide')  34 us
    psum x1, waiting for transfers between devices, per_device(): lax.psum((jnp.sum(weights, axis=-1), partial_acc), 'wide')  21.1 us
    reduce_scatter x1, waiting for transfers between devices, per_device(): lax.psum_scatter(jnp.dot(hidden, w_down, preferred_element_type=jnp.float...  20.5 us
    reduce_scatter x1, waiting for transfers between devices, per_device(): lax.psum_scatter(out_part, 'head', scatter_dimension=0, tiled=True)  20.1 us
    all_gather x1, blocking collectives, per_device(): ffn_in = lax.all_gather(normed_share, 'head', axis=0, tiled=True)  13.6 us
    psum x1, blocking collectives, per_device(): lax.psum((query_part, key_part, value_part), 'wide')  13 us
    psum x1, blocking collectives, per_device(): lax.psum((jnp.sum(weights, axis=-1), partial_acc), 'wide')  10.8 us
    pmax x1, blocking collectives, per_device(): cache_top = lax.pmax(local_top, 'wide')  10.3 us
  transfers between devices with their start and end apart: 5, of which 5 were waited for; matrix products, arithmetic and copies ran while one was open for 8% of the time, Pallas kernels for 0%

commit v1 on v0

v1 whole, which is shorter than its diff:
```python
import functools

import jax
import jax.numpy as jnp
from jax import lax
from jax.experimental import pallas as pl
from jax.experimental.pallas import tpu as pltpu
from jax.sharding import PartitionSpec as P

HEAD_WIDTH = 128
DRAFT_TOKENS = 4
SUB = 8
epsilon = 1e-05
theta_base = 500000.0
neg_large = -1e30
F32 = jnp.float32
BF16 = jnp.bfloat16
MESH = pl.DeviceIdType.MESH


def mm(a, b):
    return jnp.dot(a, b, preferred_element_type=F32)


def mm_t(a, b):
    return lax.dot_general(a, b, (((1,), (1,)), ((), ())), preferred_element_type=F32)


def layer_kernel(
    n, nh, cq, co, cg, split,
    slots_ref, lens_ref, tok, gain, fgain, cos, sin,
    wq, wk, wv, wo, wg, wu, wd, cache,
    out,
    wq_v, wk_v, wv_v, wo_v, wg_v, wu_v, wd_v, cache_v,
    x_in, tok_rows, s_q, r_q, s_kv, r_kv, ag_q, qs, ks, vs,
    s_att, r_att, ag_att, x_att, s_o, r_o, ag_r, x_f, s_ss, r_ss,
    s_g, r_g, ag_h, x_h, s_d, r_d,
    sem_wq, sem_w, sem_wg, sem_wd,
    ss_q, rs_q, ss_kv, rs_kv, ss_agq, rs_agq, ss_att, rs_att, ss_aga, rs_aga,
    ss_o, rs_o, ss_agr, rs_agr, ss_ss, rs_ss, ss_g, rs_g, ss_agh, rs_agh, ss_d, rs_d,
):
    me = lax.axis_index("wide")
    hd = lax.axis_index("head")
    total, width = tok.shape
    cols = wq.shape[0]
    qw, kw = wq.shape[1], wk.shape[1]
    ow, fw = wo.shape[1], wg.shape[1]
    kvl = kw // HEAD_WIDTH
    per = qw // kw
    rp, rh = total // n, total // nh
    ctx = cache.shape[2]
    qc, oc, gc = qw // cq, ow // co, fw // cg

    def wq_copy(c):
        at = pl.ds(pl.multiple_of(c * qc, qc), qc)
        return pltpu.make_async_copy(wq.at[:, at], wq_v.at[:, at], sem_wq.at[c])

    def wg_copy(src, dst, j, c):
        at = pl.ds(pl.multiple_of(c * gc, gc), gc)
        return pltpu.make_async_copy(src.at[:, at], dst.at[:, at], sem_wg.at[j, c])

    k_copy = pltpu.make_async_copy(wk, wk_v, sem_w.at[0])
    v_copy = pltpu.make_async_copy(wv, wv_v, sem_w.at[1])
    c_copy = pltpu.make_async_copy(cache, cache_v, sem_w.at[2])
    o_copy = pltpu.make_async_copy(wo, wo_v, sem_w.at[3])
    k_copy.start()
    v_copy.start()
    for c in range(cq):
        wq_copy(c).start()

    barrier = pltpu.get_barrier_semaphore()
    for d in range(1, n):
        pl.semaphore_signal(
            barrier, inc=1, device_id={"wide": lax.rem(me + d, n)}, device_id_type=MESH
        )
    for d in range(1, nh):
        pl.semaphore_signal(
            barrier, inc=1, device_id={"head": lax.rem(hd + d, nh)}, device_id_type=MESH
        )

    def push(axis, mine, size, d, src, dst, ssem, rsem):
        return pltpu.make_async_remote_copy(
            src_ref=src, dst_ref=dst, send_sem=ssem, recv_sem=rsem,
            device_id={axis: lax.rem(mine + d, size)}, device_id_type=MESH,
        )

    def scatter(axis, mine, size, send, recv, ssem, rsem, lead):
        made = []
        for d in range(1, size):
            peer = lax.rem(mine + d, size)
            made.append(
                push(axis, mine, size, d, send.at[lead + (peer,)], recv.at[lead + (d - 1,)],
                     ssem.at[lead + (d - 1,)], rsem.at[lead + (d - 1,)])
            )
        return made

    def gather_start(axis, mine, size, buf, ssem, rsem):
        for d in range(1, size):
            push(axis, mine, size, d, buf.at[mine], buf.at[mine], ssem.at[d - 1],
                 rsem.at[d - 1]).start()

    def gather_wait(axis, mine, size, buf, ssem, rsem):
        for d in range(1, size):
            src = lax.rem(mine + size - d, size)
            push(axis, mine, size, d, buf.at[src], buf.at[src], ssem.at[d - 1],
                 rsem.at[d - 1]).wait_recv()
            push(axis, mine, size, d, buf.at[mine], buf.at[mine], ssem.at[d - 1],
                 rsem.at[d - 1]).wait_send()

    sq = jnp.zeros((total, 1), F32)
    step = width // 8
    for c in range(8):
        part = tok[:, c * step:(c + 1) * step].astype(F32)
        sq = sq + jnp.sum(part * part, axis=1, keepdims=True)
    scale = lax.rsqrt(sq / width + epsilon)
    own = pl.ds(pl.multiple_of(me * cols, cols), cols)
    mine_f = tok[:, own].astype(F32)
    x_in[...] = (mine_f * scale * gain[:, own].astype(F32)).astype(BF16)
    for p in range(nh):
        tok_rows[p] = mine_f[p * rh:(p + 1) * rh]

    k_copy.wait()
    v_copy.wait()
    pl.semaphore_wait(barrier, n - 1 + nh - 1)
    kp = mm(x_in[...], wk_v[...])
    vp = mm(x_in[...], wv_v[...])
    for p in range(n):
        s_kv[p, :, :kw] = kp[p * rp:(p + 1) * rp]
        s_kv[p, :, kw:] = vp[p * rp:(p + 1) * rp]
    for cp in scatter("wide", me, n, s_kv, r_kv, ss_kv, rs_kv, ()):
        cp.start()

    def q_step(c, carry):
        wq_copy(c).wait()
        at = pl.ds(pl.multiple_of(c * qc, qc), qc)
        part = mm(x_in[...], wq_v[:, at])
        for p in range(n):
            s_q[c, p] = part[p * rp:(p + 1) * rp]
        for cp in scatter("wide", me, n, s_q, r_q, ss_q, rs_q, (c,)):
            cp.start()
        return carry

    lax.fori_loop(0, cq, q_step, 0)
    c_copy.start()
    o_copy.start()
    for c in range(cg):
        wg_copy(wg, wg_v, 0, c).start()
        wg_copy(wu, wu_v, 1, c).start()
    if split:
        da_copy = pltpu.make_async_copy(wd.at[:split], wq_v, sem_wd.at[0])
        da_copy.start()
    db_copy = pltpu.make_async_copy(wd.at[split:], wd_v, sem_wd.at[1])
    db_copy.start()

    cos_t, sin_t = cos[me], sin[me]

    def rotate(v):
        return v * cos_t + pltpu.roll(v, HEAD_WIDTH // 2, 1) * sin_t

    for cp in scatter("wide", me, n, s_kv, r_kv, ss_kv, rs_kv, ()):
        cp.wait()
    kv = s_kv[me]
    for d in range(n - 1):
        kv = kv + r_kv[d]
    for h in range(kvl):
        lo = h * HEAD_WIDTH
        ag_q[me, :, qw + lo:qw + lo + HEAD_WIDTH] = rotate(kv[:, lo:lo + HEAD_WIDTH]).astype(BF16)
    ag_q[me, :, qw + kw:] = kv[:, kw:].astype(BF16)
    for c in range(cq):
        for cp in scatter("wide", me, n, s_q, r_q, ss_q, rs_q, (c,)):
            cp.wait()
        qsum = s_q[c, me]
        for d in range(n - 1):
            qsum = qsum + r_q[c, d]
        for h in range(qc // HEAD_WIDTH):
            lo = h * HEAD_WIDTH
            ag_q[me, :, c * qc + lo:c * qc + lo + HEAD_WIDTH] = (
                rotate(qsum[:, lo:lo + HEAD_WIDTH]) * HEAD_WIDTH ** (-0.5)
            ).astype(BF16)
    gather_start("wide", me, n, ag_q, ss_agq, rs_agq)
    c_copy.wait()
    gather_wait("wide", me, n, ag_q, ss_agq, rs_agq)
    for p in range(n):
        rows = ag_q[p].astype(F32)
        at = slice(p * rp, (p + 1) * rp)
        for k in range(kvl):
            for g in range(per):
                lo = (k * per + g) * HEAD_WIDTH
                qs[k, g, at, :] = rows[:, lo:lo + HEAD_WIDTH]
            lo = qw + k * HEAD_WIDTH
            ks[k, at, :] = rows[:, lo:lo + HEAD_WIDTH]
            vs[k, at, :] = rows[:, lo + kw:lo + kw + HEAD_WIDTH]

    pair_rows = per * SUB
    row_of = lax.broadcasted_iota(jnp.int32, (pair_rows, ctx), 0) % SUB
    is_first = row_of < DRAFT_TOKENS
    position = me * ctx + lax.broadcasted_iota(jnp.int32, (pair_rows, ctx), 1)
    d_row = lax.broadcasted_iota(jnp.int32, (pair_rows, total), 0) % SUB
    d_col = lax.broadcasted_iota(jnp.int32, (pair_rows, total), 1)
    lane = lax.broadcasted_iota(jnp.int32, (SUB, HEAD_WIDTH), 1)
    chief = jnp.where(me == 0, 0, 1 << 20)

    def attend(t, carry):
        slot0, slot1 = slots_ref[2 * t], slots_ref[2 * t + 1]
        bound = jnp.where(is_first, lens_ref[2 * t], lens_ref[2 * t + 1])
        live = position < bound
        own_row = d_row + t * SUB
        d_live = (
            (d_col // DRAFT_TOKENS == own_row // DRAFT_TOKENS)
            & (d_col <= own_row)
            & (d_col >= chief)
        )
        for k in range(kvl):
            at = slice(k * HEAD_WIDTH, (k + 1) * HEAD_WIDTH)
            q = qs[k, :, pl.ds(pl.multiple_of(t * SUB, SUB), SUB), :]
            q = q.reshape(pair_rows, HEAD_WIDTH).astype(BF16)
            sc = jnp.where(
                is_first, mm_t(q, cache_v[0, slot0, :, at]), mm_t(q, cache_v[0, slot1, :, at])
            )
            sc = jnp.where(live, sc, neg_large)
            sd = jnp.where(d_live, mm_t(q, ks[k].astype(BF16)), neg_large)
            top = jnp.maximum(
                jnp.max(sc, axis=1, keepdims=True), jnp.max(sd, axis=1, keepdims=True)
            )
            w = jnp.where(live, jnp.exp(sc - top), 0.0)
            u = jnp.where(d_live, jnp.exp(sd - top), 0.0)
            den = jnp.sum(w, axis=1, keepdims=True) + jnp.sum(u, axis=1, keepdims=True)
            acc = (
                mm(jnp.where(is_first, w, 0.0).astype(BF16), cache_v[1, slot0, :, at])
                + mm(jnp.where(is_first, 0.0, w).astype(BF16), cache_v[1, slot1, :, at])
                + mm(u.astype(BF16), vs[k].astype(BF16))
            )
            acc = acc.reshape(per, SUB, HEAD_WIDTH)
            packed = jnp.zeros((SUB, HEAD_WIDTH), F32)
            for g in range(per):
                rows = slice(g * SUB, (g + 1) * SUB)
                packed = jnp.where(lane == g, top[rows], packed)
                packed = jnp.where(lane == per + g, den[rows], packed)
            for o in range(SUB // rp):
                at_p = t * (SUB // rp) + o
                rows = slice(o * rp, (o + 1) * rp)
                for g in range(per):
                    s_att[at_p, k, g] = acc[g, rows]
                s_att[at_p, k, per] = packed[rows]
        return carry

    lax.fori_loop(0, total // SUB, attend, 0)
    att_moves = scatter("wide", me, n, s_att, r_att, ss_att, rs_att, ())
    for cp in att_moves:
        cp.start()
    for cp in att_moves:
        cp.wait()
    for k in range(kvl):
        stats = [s_att[me, k, per]] + [r_att[d, k, per] for d in range(n - 1)]
        top = stats[0]
        for st in stats[1:]:
            top = jnp.maximum(top, st)
        shrink = [jnp.exp(st - top) for st in stats]
        for g in range(per):
            num = jnp.zeros((rp, HEAD_WIDTH), F32)
            den = jnp.zeros((rp, 1), F32)
            for i in range(n):
                f = shrink[i][:, g:g + 1]
                part = s_att[me, k, g] if i == 0 else r_att[i - 1, k, g]
                num = num + f * part
                den = den + f * stats[i][:, per + g:per + g + 1]
            lo = (k * per + g) * HEAD_WIDTH
            ag_att[me, :, lo:lo + HEAD_WIDTH] = (num / den).astype(BF16)
    gather_start("wide", me, n, ag_att, ss_aga, rs_aga)
    o_copy.wait()
    gather_wait("wide", me, n, ag_att, ss_aga, rs_aga)
    x_att[...] = jnp.concatenate([ag_att[p].astype(F32) for p in range(n)], axis=0).astype(BF16)

    def o_step(c, carry):
        at = pl.ds(pl.multiple_of(c * oc, oc), oc)
        part = mm(x_att[...], wo_v[:, at])
        for p in range(nh):
            s_o[c, p] = part[p * rh:(p + 1) * rh]
        for cp in scatter("head", hd, nh, s_o, r_o, ss_o, rs_o, (c,)):
            cp.start()
        return carry

    lax.fori_loop(0, co, o_step, 0)
    for c in range(co):
        for cp in scatter("head", hd, nh, s_o, r_o, ss_o, rs_o, (c,)):
            cp.wait()
        osum = s_o[c, hd]
        for d in range(nh - 1):
            osum = osum + r_o[c, d]
        at = slice(c * oc, (c + 1) * oc)
        ag_r[hd, :, at] = (tok_rows[hd, :, at] + osum).astype(BF16)
    gather_start("head", hd, nh, ag_r, ss_agr, rs_agr)
    gather_wait("head", hd, nh, ag_r, ss_agr, rs_agr)
    resid = jnp.concatenate([ag_r[p].astype(F32) for p in range(nh)], axis=0)
    x_f[...] = (resid * fgain[...].astype(F32)).astype(BF16)
    squares = jnp.broadcast_to(jnp.sum(resid * resid, axis=1, keepdims=True), (total, HEAD_WIDTH))
    for p in range(n):
        s_ss[p] = squares[p * rp:(p + 1) * rp]
    ss_moves = scatter("wide", me, n, s_ss, r_ss, ss_ss, rs_ss, ())
    for cp in ss_moves:
        cp.start()

    def g_step(c, carry):
        wg_copy(wg, wg_v, 0, c).wait()
        wg_copy(wu, wu_v, 1, c).wait()
        at = pl.ds(pl.multiple_of(c * gc, gc), gc)
        gate = mm(x_f[...], wg_v[:, at])
        up = mm(x_f[...], wu_v[:, at])
        for p in range(n):
            s_g[c, p, 0] = gate[p * rp:(p + 1) * rp]
            s_g[c, p, 1] = up[p * rp:(p + 1) * rp]
        for cp in scatter("wide", me, n, s_g, r_g, ss_g, rs_g, (c,)):
            cp.start()
        return carry

    lax.fori_loop(0, cg, g_step, 0)
    for cp in ss_moves:
        cp.wait()
    sq = s_ss[me]
    for d in range(n - 1):
        sq = sq + r_ss[d]
    scale = lax.rsqrt(sq[:, :1] / width + epsilon)
    for c in range(cg):
        for cp in scatter("wide", me, n, s_g, r_g, ss_g, rs_g, (c,)):
            cp.wait()
        gate, up = s_g[c, me, 0], s_g[c, me, 1]
        for d in range(n - 1):
            gate = gate + r_g[c, d, 0]
            up = up + r_g[c, d, 1]
        gate = gate * scale
        up = up * scale
        ag_h[me, :, c * gc:(c + 1) * gc] = (gate / (1.0 + jnp.exp(-gate)) * up).astype(BF16)
    gather_start("wide", me, n, ag_h, ss_agh, rs_agh)
    if split:
        da_copy.wait()
    db_copy.wait()
    gather_wait("wide", me, n, ag_h, ss_agh, rs_agh)
    x_h[...] = jnp.concatenate([ag_h[p].astype(F32) for p in range(n)], axis=0).astype(BF16)

    def d_step(c, carry):
        at = pl.ds(pl.multiple_of(c * oc, oc), oc)
        part = mm(x_h[:, split:], wd_v[:, at])
        if split:
            part = part + mm(x_h[:, :split], wq_v[:, at])
        for p in range(nh):
            s_d[c, p] = part[p * rh:(p + 1) * rh]
        for cp in scatter("head", hd, nh, s_d, r_d, ss_d, rs_d, (c,)):
            cp.start()
        return carry

    lax.fori_loop(0, co, d_step, 0)
    for c in range(co):
        for cp in scatter("head", hd, nh, s_d, r_d, ss_d, rs_d, (c,)):
            cp.wait()
        dsum = s_d[c, hd]
        for d in range(nh - 1):
            dsum = dsum + r_d[c, d]
        at = slice(c * oc, (c + 1) * oc)
        out[:, at] = (ag_r[hd, :, at].astype(F32) + dsum).astype(BF16)


def chunks_of(columns, wanted, peers):
    if peers > 4 or columns % (wanted * HEAD_WIDTH):
        return 1
    return wanted


def per_device(
    n, nh,
    tokens, attn_gain, ffn_gain, w_query, key_matrix, value_matrix,
    w_out, w_gate, w_up, w_down, kv_cache, lengths, slots,
):
    total, width = tokens.shape
    cols, qw = w_query.shape
    kw = key_matrix.shape[1]
    ow, fw = w_out.shape[1], w_gate.shape[1]
    kvl, per = kw // HEAD_WIDTH, qw // kw
    rp, rh = total // n, total // nh
    cq, co = chunks_of(qw, 4, n), chunks_of(ow, 4, nh)
    cg = chunks_of(fw, 7, n)
    qc, oc, gc = qw // cq, ow // co, fw // cg
    split = cols if w_down.shape[1] == qw and w_down.shape[0] > cols else 0
    positions = (
        jnp.repeat(lengths, DRAFT_TOKENS) + jnp.arange(total, dtype=jnp.int32) % DRAFT_TOKENS
    ).astype(F32)
    exponent = jnp.arange(HEAD_WIDTH // 2, dtype=F32) * (2.0 / HEAD_WIDTH)
    angles = positions[:, None] * (theta_base ** (-exponent))[None, :]
    cosine, sine = jnp.cos(angles), jnp.sin(angles)
    cos2 = jnp.concatenate([cosine, cosine], axis=1).reshape(n, rp, HEAD_WIDTH)
    sin2 = jnp.concatenate([-sine, sine], axis=1).reshape(n, rp, HEAD_WIDTH)
    vmem = pl.BlockSpec(memory_space=pltpu.VMEM)
    smem = pl.BlockSpec(memory_space=pltpu.SMEM)
    hbm = pl.BlockSpec(memory_space=pl.ANY)
    V = pltpu.VMEM

    def sems(*shape):
        return [pltpu.SemaphoreType.DMA(shape)] * 2

    scratch = [
        V(w_query.shape, BF16), V(key_matrix.shape, BF16), V(value_matrix.shape, BF16),
        V(w_out.shape, BF16), V(w_gate.shape, BF16), V(w_up.shape, BF16),
        V((w_down.shape[0] - split, w_down.shape[1]), BF16), V(kv_cache.shape, BF16),
        V((total, cols), BF16), V((nh, rh, cols), F32),
        V((cq, n, rp, qc), F32), V((cq, n - 1, rp, qc), F32),
        V((n, rp, 2 * kw), F32), V((n - 1, rp, 2 * kw), F32),
        V((n, rp, qw + 2 * kw), BF16),
        V((kvl, per, total, HEAD_WIDTH), F32),
        V((kvl, total, HEAD_WIDTH), F32), V((kvl, total, HEAD_WIDTH), F32),
        V((n, kvl, per + 1, rp, HEAD_WIDTH), F32), V((n - 1, kvl, per + 1, rp, HEAD_WIDTH), F32),
        V((n, rp, qw), BF16), V((total, qw), BF16),
        V((co, nh, rh, oc), F32), V((co, nh - 1, rh, oc), F32),
        V((nh, rh, ow), BF16), V((total, ow), BF16),
        V((n, rp, HEAD_WIDTH), F32), V((n - 1, rp, HEAD_WIDTH), F32),
        V((cg, n, 2, rp, gc), F32), V((cg, n - 1, 2, rp, gc), F32),
        V((n, rp, fw), BF16), V((total, fw), BF16),
        V((co, nh, rh, oc), F32), V((co, nh - 1, rh, oc), F32),
        pltpu.SemaphoreType.DMA((cq,)), pltpu.SemaphoreType.DMA((4,)),
        pltpu.SemaphoreType.DMA((2, cg)), pltpu.SemaphoreType.DMA((2,)),
        *sems(cq, n - 1), *sems(n - 1), *sems(n - 1), *sems(n - 1), *sems(n - 1),
        *sems(co, nh - 1), *sems(nh - 1), *sems(n - 1), *sems(cg, n - 1),
        *sems(n - 1), *sems(co, nh - 1),
    ]
    return pl.pallas_call(
        functools.partial(layer_kernel, n, nh, cq, co, cg, split),
        out_shape=jax.ShapeDtypeStruct((rh, ow), BF16),
        in_specs=[smem, smem] + [vmem] * 5 + [hbm] * 8,
        out_specs=vmem,
        scratch_shapes=scratch,
        compiler_params=pltpu.CompilerParams(
            collective_id=0, has_side_effects=True, vmem_limit_bytes=67043328
        ),
    )(
        slots, lengths, tokens, attn_gain[None, :], ffn_gain[None, :], cos2, sin2,
        w_query, key_matrix, value_matrix, w_out, w_gate, w_up, w_down, kv_cache,
    )


def solution(mesh):
    in_specs = (
        P("grp", None),
        P(),
        P("wide"),
        P("wide", "head"),
        P("wide", "head"),
        P("wide", "head"),
        P("head", "wide"),
        P("wide", "head"),
        P("wide", "head"),
        P("head", "wide"),
        P(None, "grp", "wide", "head"),
        P("grp"),
        P("grp"),
    )
    return jax.shard_map(
        functools.partial(per_device, mesh.shape["wide"], mesh.shape["head"]),
        mesh=mesh, in_specs=in_specs, out_specs=P(("grp", "head"), "wide"), check_vma=False,
    )
```

time: 237 us -> 75.8 us (0.32)
  waiting for transfers between devices: 99.8 us -> 0 us
  Pallas kernels: 0 us -> 69.7 us
  blocking collectives: 53.3 us -> 0 us
  matrix products: 42.7 us -> 0 us
  between operations: 13.4 us -> 0.02 us
  local copies, waits for them, and re-layouts: 15.8 us -> 4.9 us
  other arithmetic: 10.5 us -> 0.86 us
    pallas_call x0 -> x1, Pallas kernels: none -> 69.7 us  [per_device(): pl.pallas_call(functools.partial(layer_kernel, n, nh, cq, co, cg, split),...]
    psum x3 -> x0, waiting for transfers between devices: 59.2 us -> none  [the longest x1 34 us: per_device(): gate_sum, up_sum = lax.psum((gate_part, up_part), 'wide')]
    dot_general x11 -> x0, matrix products: 42.7 us -> none  [the longest x1 8.86 us: per_device(): jnp.dot(hidden, w_down, preferred_element_type=jnp.float32)]
    reduce_scatter x2 -> x0, waiting for transfers between devices: 40.6 us -> none  [the longest x1 20.5 us: per_device(): lax.psum_scatter(jnp.dot(hidden, w_down, preferred_element_type=jnp.float...]
    psum x3 -> x0, blocking collectives: 29.5 us -> none  [the longest x1 13 us: per_device(): lax.psum((query_part, key_part, value_part), 'wide')]
    all_gather x1 -> x0, blocking collectives: 13.6 us -> none  [per_device(): ffn_in = lax.all_gather(normed_share, 'head', axis=0, tiled=True)]
    pmax x1 -> x0, blocking collectives: 10.3 us -> none  [per_device(): cache_top = lax.pmax(local_top, 'wide')]
    slice x3 -> x0, local copies, waits for them, and re-layouts: 9.1 us -> none  [the longest x2 6.22 us: per_device(): keys_local = ordered[0].reshape(requests, ctx_local, kv_local, HEAD_WIDTH)]
  transfers between devices with their start and end apart: 5 -> 0, of which waited for: 5 -> 0; matrix products, arithmetic and copies ran while one was open for 8% -> 0% of each run, Pallas kernels for 0% -> 0%
where the time goes in v1:
time: 75.8 us; the launch traced here: 75.5 us
  Pallas kernels  69.7 us (92%)
  local copies, waits for them, and re-layouts  4.9 us (6%)
  other arithmetic  0.86 us (1%)
    pallas_call x1, Pallas kernels, per_device(): pl.pallas_call(functools.partial(layer_kernel, n, nh, cq, co, cg, split),...  69.7 us

profile of v1, /device:TPU:0, one launch (start us, length us, event | category | flops | bytes accessed | tf_op | source)
XLA Modules:
  0.0 75.5 jit_solution(236120565305272144)
XLA Ops:
  0.0 0.7 broadcast_in_dim.17
  0.7 0.1 broadcast_in_dim.18
  0.8 0.1 broadcast_in_dim.19
  0.9 0.1 fusion
  1.1 0.7 pad_maximum_fusion
  1.8 1.3 %broadcast_in_dim.15.gain = bf16[1,8192]{1,0:T(2,128)(2,1)} reshape(bf16[8192]{0:T(1024)(128)(2,1)} %param.14) | data formatting | bytes 32768 | tf_op jit(solution)/shard_map/broadcast_in_dim | solution.py:433
  3.1 1.3 %broadcast_in_dim.16.fgain = bf16[1,2048]{1,0:T(2,128)(2,1)} reshape(bf16[2048]{0:T(1024)(128)(2,1)} %param.15) | data formatting | bytes 8192 | tf_op jit(solution)/shard_map/broadcast_in_dim | solution.py:433
  4.4 69.7 %shard_map.127 = bf16[8,2048]{1,0:T(8,128)(2,1)} custom-call(s32[8]{0:T(128)} %slots_ref.1, s32[8]{0:T(128)} %lens_ref.1, bf16[32,8192]{1,0:T(8,128)(2,1)} %tok.1, bf16[1,8192]{1,0:T(2,128)(2,1)} %broadcast_in_dim.15.gain, bf16[1,2048]{1,0:T(2,128)(2,1)} %broadcast_in_dim.16.fgain, f32[4,8,128]{2,1,0:T(8,128)} %get-tuple-element.8.cos, ...), custom_call_target="tpu_custom_call" | custom-call | tf_op jit(solution)/shard_map/pallas_call | solution.py:423
  74.1 1.4 %copy.15 = bf16[8,2048]{1,0:T(8,128)(2,1)} copy(bf16[8,2048]{1,0:T(8,128)(2,1)} %shard_map.127) | data formatting | bytes 65536
  (2 shorter events, 0.0 us)

commit v2 on v1

--- a/solution.py
+++ b/solution.py
@@ -10,6 +10,7 @@
 HEAD_WIDTH = 128
 DRAFT_TOKENS = 4
 SUB = 8
+LAG = 2
 epsilon = 1e-05
 theta_base = 500000.0
 neg_large = -1e30
@@ -32,11 +33,11 @@
     wq, wk, wv, wo, wg, wu, wd, cache,
     out,
     wq_v, wk_v, wv_v, wo_v, wg_v, wu_v, wd_v, cache_v,
-    x_in, tok_rows, s_q, r_q, s_kv, r_kv, ag_q, qs, ks, vs,
-    s_att, r_att, ag_att, x_att, s_o, r_o, ag_r, x_f, s_ss, r_ss,
+    x_in, tok_rows, s_q, r_q, s_kv, r_kv, ag_q, ag_kv, qs, ks, vs,
+    s_att, r_att, ag_att, x_att, s_o, r_o, ag_r, x_f, s_ss, r_ss, row_scale,
     s_g, r_g, ag_h, x_h, s_d, r_d,
     sem_wq, sem_w, sem_wg, sem_wd,
-    ss_q, rs_q, ss_kv, rs_kv, ss_agq, rs_agq, ss_att, rs_att, ss_aga, rs_aga,
+    ss_q, rs_q, ss_kv, rs_kv, ss_agq, rs_agq, ss_agkv, rs_agkv, ss_att, rs_att, ss_aga, rs_aga,
     ss_o, rs_o, ss_agr, rs_agr, ss_ss, rs_ss, ss_g, rs_g, ss_agh, rs_agh, ss_d, rs_d,
 ):
     me = lax.axis_index("wide")
@@ -94,18 +95,40 @@
             )
         return made
 
-    def gather_start(axis, mine, size, buf, ssem, rsem):
+    def gather_start(axis, mine, size, buf, ssem, rsem, lead=()):
         for d in range(1, size):
-            push(axis, mine, size, d, buf.at[mine], buf.at[mine], ssem.at[d - 1],
-                 rsem.at[d - 1]).start()
-
-    def gather_wait(axis, mine, size, buf, ssem, rsem):
+            own_at, sem_at = lead + (mine,), lead + (d - 1,)
+            push(axis, mine, size, d, buf.at[own_at], buf.at[own_at], ssem.at[sem_at],
+                 rsem.at[sem_at]).start()
+
+    def gather_wait(axis, mine, size, buf, ssem, rsem, lead=()):
         for d in range(1, size):
-            src = lax.rem(mine + size - d, size)
-            push(axis, mine, size, d, buf.at[src], buf.at[src], ssem.at[d - 1],
-                 rsem.at[d - 1]).wait_recv()
-            push(axis, mine, size, d, buf.at[mine], buf.at[mine], ssem.at[d - 1],
-                 rsem.at[d - 1]).wait_send()
+            own_at, sem_at = lead + (mine,), lead + (d - 1,)
+            src_at = lead + (lax.rem(mine + size - d, size),)
+            push(axis, mine, size, d, buf.at[src_at], buf.at[src_at], ssem.at[sem_at],
+                 rsem.at[sem_at]).wait_recv()
+            push(axis, mine, size, d, buf.at[own_at], buf.at[own_at], ssem.at[sem_at],
+                 rsem.at[sem_at]).wait_send()
+
+    def staged(count, produce, settle, between=None):
+        lag = min(LAG, count)
+
+        def first(c, carry):
+            produce(c)
+            return carry
+
+        def both(c, carry):
+            produce(c)
+            settle(c - lag)
+            return carry
+
+        lax.fori_loop(0, lag, first, 0)
+        if between is not None:
+            between()
+        if count > lag:
+            lax.fori_loop(lag, count, both, 0)
+        for c in range(count - lag, count):
+            settle(c)
 
     sq = jnp.zeros((total, 1), F32)
     step = width // 8
@@ -115,7 +138,7 @@
     scale = lax.rsqrt(sq / width + epsilon)
     own = pl.ds(pl.multiple_of(me * cols, cols), cols)
     mine_f = tok[:, own].astype(F32)
-    x_in[...] = (mine_f * scale * gain[:, own].astype(F32)).astype(BF16)
+    x_in[...] = (mine_f * scale * gain[:, own]).astype(BF16)
     for p in range(nh):
         tok_rows[p] = mine_f[p * rh:(p + 1) * rh]
 
@@ -130,7 +153,12 @@
     for cp in scatter("wide", me, n, s_kv, r_kv, ss_kv, rs_kv, ()):
         cp.start()
 
-    def q_step(c, carry):
+    cos_t, sin_t = cos[me], sin[me]
+
+    def rotate(v):
+        return v * cos_t + pltpu.roll(v, HEAD_WIDTH // 2, 1) * sin_t
+
+    def q_step(c):
         wq_copy(c).wait()
         at = pl.ds(pl.multiple_of(c * qc, qc), qc)
         part = mm(x_in[...], wq_v[:, at])
@@ -138,35 +166,8 @@
             s_q[c, p] = part[p * rp:(p + 1) * rp]
         for cp in scatter("wide", me, n, s_q, r_q, ss_q, rs_q, (c,)):
             cp.start()
-        return carry
-
-    lax.fori_loop(0, cq, q_step, 0)
-    c_copy.start()
-    o_copy.start()
-    for c in range(cg):
-        wg_copy(wg, wg_v, 0, c).start()
-        wg_copy(wu, wu_v, 1, c).start()
-    if split:
-        da_copy = pltpu.make_async_copy(wd.at[:split], wq_v, sem_wd.at[0])
-        da_copy.start()
-    db_copy = pltpu.make_async_copy(wd.at[split:], wd_v, sem_wd.at[1])
-    db_copy.start()
-
-    cos_t, sin_t = cos[me], sin[me]
-
-    def rotate(v):
-        return v * cos_t + pltpu.roll(v, HEAD_WIDTH // 2, 1) * sin_t
-
-    for cp in scatter("wide", me, n, s_kv, r_kv, ss_kv, rs_kv, ()):
-        cp.wait()
-    kv = s_kv[me]
-    for d in range(n - 1):
-        kv = kv + r_kv[d]
-    for h in range(kvl):
-        lo = h * HEAD_WIDTH
-        ag_q[me, :, qw + lo:qw + lo + HEAD_WIDTH] = rotate(kv[:, lo:lo + HEAD_WIDTH]).astype(BF16)
-    ag_q[me, :, qw + kw:] = kv[:, kw:].astype(BF16)
-    for c in range(cq):
+
+    def q_settle(c):
         for cp in scatter("wide", me, n, s_q, r_q, ss_q, rs_q, (c,)):
             cp.wait()
         qsum = s_q[c, me]
@@ -174,20 +175,46 @@
             qsum = qsum + r_q[c, d]
         for h in range(qc // HEAD_WIDTH):
             lo = h * HEAD_WIDTH
-            ag_q[me, :, c * qc + lo:c * qc + lo + HEAD_WIDTH] = (
+            ag_q[c, me, :, lo:lo + HEAD_WIDTH] = (
                 rotate(qsum[:, lo:lo + HEAD_WIDTH]) * HEAD_WIDTH ** (-0.5)
             ).astype(BF16)
-    gather_start("wide", me, n, ag_q, ss_agq, rs_agq)
+        gather_start("wide", me, n, ag_q, ss_agq, rs_agq, (c,))
+
+    def kv_settle():
+        for cp in scatter("wide", me, n, s_kv, r_kv, ss_kv, rs_kv, ()):
+            cp.wait()
+        kv = s_kv[me]
+        for d in range(n - 1):
+            kv = kv + r_kv[d]
+        for h in range(kvl):
+            lo = h * HEAD_WIDTH
+            ag_kv[me, :, lo:lo + HEAD_WIDTH] = rotate(kv[:, lo:lo + HEAD_WIDTH]).astype(BF16)
+        ag_kv[me, :, kw:] = kv[:, kw:].astype(BF16)
+        gather_start("wide", me, n, ag_kv, ss_agkv, rs_agkv)
+        c_copy.start()
+        o_copy.start()
+        for c in range(cg):
+            wg_copy(wg, wg_v, 0, c).start()
+            wg_copy(wu, wu_v, 1, c).start()
+        db_copy.start()
+
+    db_copy = pltpu.make_async_copy(wd.at[split:], wd_v, sem_wd.at[1])
+    staged(cq, q_step, q_settle, kv_settle)
+    if split:
+        da_copy = pltpu.make_async_copy(wd.at[:split], wq_v, sem_wd.at[0])
+        da_copy.start()
     c_copy.wait()
-    gather_wait("wide", me, n, ag_q, ss_agq, rs_agq)
+    gather_wait("wide", me, n, ag_kv, ss_agkv, rs_agkv)
+    for c in range(cq):
+        gather_wait("wide", me, n, ag_q, ss_agq, rs_agq, (c,))
     for p in range(n):
-        rows = ag_q[p].astype(F32)
         at = slice(p * rp, (p + 1) * rp)
+        for h in range(kvl * per):
+            c, lo = divmod(h * HEAD_WIDTH, qc)
+            qs[h // per, h % per, at, :] = ag_q[c, p, :, lo:lo + HEAD_WIDTH].astype(F32)
+        rows = ag_kv[p].astype(F32)
         for k in range(kvl):
-            for g in range(per):
-                lo = (k * per + g) * HEAD_WIDTH
-                qs[k, g, at, :] = rows[:, lo:lo + HEAD_WIDTH]
-            lo = qw + k * HEAD_WIDTH
+            lo = k * HEAD_WIDTH
             ks[k, at, :] = rows[:, lo:lo + HEAD_WIDTH]
             vs[k, at, :] = rows[:, lo + kw:lo + kw + HEAD_WIDTH]
 
@@ -271,36 +298,40 @@
     gather_wait("wide", me, n, ag_att, ss_aga, rs_aga)
     x_att[...] = jnp.concatenate([ag_att[p].astype(F32) for p in range(n)], axis=0).astype(BF16)
 
-    def o_step(c, carry):
+    def o_step(c):
         at = pl.ds(pl.multiple_of(c * oc, oc), oc)
         part = mm(x_att[...], wo_v[:, at])
         for p in range(nh):
             s_o[c, p] = part[p * rh:(p + 1) * rh]
         for cp in scatter("head", hd, nh, s_o, r_o, ss_o, rs_o, (c,)):
             cp.start()
-        return carry
-
-    lax.fori_loop(0, co, o_step, 0)
-    for c in range(co):
+
+    def o_settle(c):
         for cp in scatter("head", hd, nh, s_o, r_o, ss_o, rs_o, (c,)):
             cp.wait()
         osum = s_o[c, hd]
         for d in range(nh - 1):
             osum = osum + r_o[c, d]
+        at = pl.ds(pl.multiple_of(c * oc, oc), oc)
+        ag_r[c, hd] = (tok_rows[hd, :, at] + osum).astype(BF16)
+        gather_start("head", hd, nh, ag_r, ss_agr, rs_agr, (c,))
+
+    staged(co, o_step, o_settle)
+    square = jnp.zeros((total, 1), F32)
+    for c in range(co):
+        gather_wait("head", hd, nh, ag_r, ss_agr, rs_agr, (c,))
+        resid = jnp.concatenate([ag_r[c, p].astype(F32) for p in range(nh)], axis=0)
         at = slice(c * oc, (c + 1) * oc)
-        ag_r[hd, :, at] = (tok_rows[hd, :, at] + osum).astype(BF16)
-    gather_start("head", hd, nh, ag_r, ss_agr, rs_agr)
-    gather_wait("head", hd, nh, ag_r, ss_agr, rs_agr)
-    resid = jnp.concatenate([ag_r[p].astype(F32) for p in range(nh)], axis=0)
-    x_f[...] = (resid * fgain[...].astype(F32)).astype(BF16)
-    squares = jnp.broadcast_to(jnp.sum(resid * resid, axis=1, keepdims=True), (total, HEAD_WIDTH))
+        x_f[:, at] = (resid * fgain[:, at]).astype(BF16)
+        square = square + jnp.sum(resid * resid, axis=1, keepdims=True)
+    squares = jnp.broadcast_to(square, (total, HEAD_WIDTH))
     for p in range(n):
         s_ss[p] = squares[p * rp:(p + 1) * rp]
     ss_moves = scatter("wide", me, n, s_ss, r_ss, ss_ss, rs_ss, ())
     for cp in ss_moves:
         cp.start()
 
-    def g_step(c, carry):
+    def g_step(c):
         wg_copy(wg, wg_v, 0, c).wait()
         wg_copy(wu, wu_v, 1, c).wait()
         at = pl.ds(pl.multiple_of(c * gc, gc), gc)
@@ -311,33 +342,39 @@
             s_g[c, p, 1] = up[p * rp:(p + 1) * rp]
         for cp in scatter("wide", me, n, s_g, r_g, ss_g, rs_g, (c,)):
             cp.start()
-        return carry
-
-    lax.fori_loop(0, cg, g_step, 0)
-    for cp in ss_moves:
-        cp.wait()
-    sq = s_ss[me]
-    for d in range(n - 1):
-        sq = sq + r_ss[d]
-    scale = lax.rsqrt(sq[:, :1] / width + epsilon)
-    for c in range(cg):
+
+    def ss_settle():
+        for cp in ss_moves:
+            cp.wait()
+        sq = s_ss[me]
+        for d in range(n - 1):
+            sq = sq + r_ss[d]
+        row_scale[...] = lax.rsqrt(sq / width + epsilon)
+
+    def g_settle(c):
         for cp in scatter("wide", me, n, s_g, r_g, ss_g, rs_g, (c,)):
             cp.wait()
         gate, up = s_g[c, me, 0], s_g[c, me, 1]
         for d in range(n - 1):
             gate = gate + r_g[c, d, 0]
             up = up + r_g[c, d, 1]
+        scale = row_scale[...][:, :1]
         gate = gate * scale
         up = up * scale
-        ag_h[me, :, c * gc:(c + 1) * gc] = (gate / (1.0 + jnp.exp(-gate)) * up).astype(BF16)
-    gather_start("wide", me, n, ag_h, ss_agh, rs_agh)
+        ag_h[c, me] = (gate / (1.0 + jnp.exp(-gate)) * up).astype(BF16)
+        gather_start("wide", me, n, ag_h, ss_agh, rs_agh, (c,))
+
+    staged(cg, g_step, g_settle, ss_settle)
     if split:
         da_copy.wait()
     db_copy.wait()
-    gather_wait("wide", me, n, ag_h, ss_agh, rs_agh)
-    x_h[...] = jnp.concatenate([ag_h[p].astype(F32) for p in range(n)], axis=0).astype(BF16)
-
-    def d_step(c, carry):
+    for c in range(cg):
+        gather_wait("wide", me, n, ag_h, ss_agh, rs_agh, (c,))
+        x_h[:, c * gc:(c + 1) * gc] = jnp.concatenate(
+            [ag_h[c, p].astype(F32) for p in range(n)], axis=0
+        ).astype(BF16)
+
+    def d_step(c):
         at = pl.ds(pl.multiple_of(c * oc, oc), oc)
         part = mm(x_h[:, split:], wd_v[:, at])
         if split:
@@ -346,17 +383,17 @@
             s_d[c, p] = part[p * rh:(p + 1) * rh]
         for cp in scatter("head", hd, nh, s_d, r_d, ss_d, rs_d, (c,)):
             cp.start()
-        return carry
-
-    lax.fori_loop(0, co, d_step, 0)
-    for c in range(co):
+
+    def d_settle(c):
         for cp in scatter("head", hd, nh, s_d, r_d, ss_d, rs_d, (c,)):
             cp.wait()
         dsum = s_d[c, hd]
         for d in range(nh - 1):
             dsum = dsum + r_d[c, d]
-        at = slice(c * oc, (c + 1) * oc)
-        out[:, at] = (ag_r[hd, :, at].astype(F32) + dsum).astype(BF16)
+        at = pl.ds(pl.multiple_of(c * oc, oc), oc)
+        out[:, at] = (ag_r[c, hd].astype(F32) + dsum).astype(BF16)
+
+    staged(co, d_step, d_settle)
 
 
 def chunks_of(columns, wanted, peers):
@@ -403,22 +440,23 @@
         V((total, cols), BF16), V((nh, rh, cols), F32),
         V((cq, n, rp, qc), F32), V((cq, n - 1, rp, qc), F32),
         V((n, rp, 2 * kw), F32), V((n - 1, rp, 2 * kw), F32),
-        V((n, rp, qw + 2 * kw), BF16),
+        V((cq, n, rp, qc), BF16), V((n, rp, 2 * kw), BF16),
         V((kvl, per, total, HEAD_WIDTH), F32),
         V((kvl, total, HEAD_WIDTH), F32), V((kvl, total, HEAD_WIDTH), F32),
         V((n, kvl, per + 1, rp, HEAD_WIDTH), F32), V((n - 1, kvl, per + 1, rp, HEAD_WIDTH), F32),
         V((n, rp, qw), BF16), V((total, qw), BF16),
         V((co, nh, rh, oc), F32), V((co, nh - 1, rh, oc), F32),
-        V((nh, rh, ow), BF16), V((total, ow), BF16),
+        V((co, nh, rh, oc), BF16), V((total, ow), BF16),
         V((n, rp, HEAD_WIDTH), F32), V((n - 1, rp, HEAD_WIDTH), F32),
+        V((rp, HEAD_WIDTH), F32),
         V((cg, n, 2, rp, gc), F32), V((cg, n - 1, 2, rp, gc), F32),
-        V((n, rp, fw), BF16), V((total, fw), BF16),
+        V((cg, n, rp, gc), BF16), V((total, fw), BF16),
         V((co, nh, rh, oc), F32), V((co, nh - 1, rh, oc), F32),
         pltpu.SemaphoreType.DMA((cq,)), pltpu.SemaphoreType.DMA((4,)),
         pltpu.SemaphoreType.DMA((2, cg)), pltpu.SemaphoreType.DMA((2,)),
-        *sems(cq, n - 1), *sems(n - 1), *sems(n - 1), *sems(n - 1), *sems(n - 1),
-        *sems(co, nh - 1), *sems(nh - 1), *sems(n - 1), *sems(cg, n - 1),
-        *sems(n - 1), *sems(co, nh - 1),
+        *sems(cq, n - 1), *sems(n - 1), *sems(cq, n - 1), *sems(n - 1), *sems(n - 1), *sems(n - 1),
+        *sems(co, nh - 1), *sems(co, nh - 1), *sems(n - 1), *sems(cg, n - 1),
+        *sems(cg, n - 1), *sems(co, nh - 1),
     ]
     return pl.pallas_call(
         functools.partial(layer_kernel, n, nh, cq, co, cg, split),
@@ -430,7 +468,7 @@
             collective_id=0, has_side_effects=True, vmem_limit_bytes=67043328
         ),
     )(
-        slots, lengths, tokens, attn_gain[None, :], ffn_gain[None, :], cos2, sin2,
+        slots, lengths, tokens, attn_gain.astype(F32)[None, :], ffn_gain.astype(F32)[None, :], cos2, sin2,
         w_query, key_matrix, value_matrix, w_out, w_gate, w_up, w_down, kv_cache,
     )
 

time: 75.8 us -> 80.5 us (1.062)
  Pallas kernels: 69.7 us -> 74.4 us
  local copies, waits for them, and re-layouts: 4.9 us -> 2.27 us
  other arithmetic: 0.86 us -> 3.47 us
    pallas_call x1, Pallas kernels: 69.7 us -> 74.4 us  [per_device(): pl.pallas_call(functools.partial(layer_kernel, n, nh, cq, co, cg, split),...]
    broadcast_in_dim x2 -> x0, local copies, waits for them, and re-layouts: 2.64 us -> none  [the longest x1 1.35 us: per_device(): attn_gain[None, :]]
    broadcast_in_dim x0 -> x2, other arithmetic: none -> 2.62 us  [the longest x1 1.33 us: per_device(): attn_gain.astype(F32)[None, :]]
where the time goes in v2:
time: 80.5 us; the launch traced here: 80.2 us
  Pallas kernels  74.4 us (92%)
  other arithmetic  3.47 us (4%)
  local copies, waits for them, and re-layouts  2.27 us (3%)
    pallas_call x1, Pallas kernels, per_device(): pl.pallas_call(functools.partial(layer_kernel, n, nh, cq, co, cg, split),...  74.4 us

profile of v2, /device:TPU:0, one launch (start us, length us, event | category | flops | bytes accessed | tf_op | source)
XLA Modules:
  0.0 80.2 jit_solution(13574438315941476376)
XLA Ops:
  0.0 0.7 broadcast_in_dim.23
  0.7 0.1 broadcast_in_dim.24
  0.8 0.1 broadcast_in_dim.25
  0.9 0.1 fusion
  1.1 0.7 pad_maximum_fusion
  1.8 1.3 %broadcast_in_dim.26 = f32[8192]{0:T(1024)} convert(bf16[8192]{0:T(1024)(128)(2,1)} %param.14) | non-fusion elementwise | flops 8192 | bytes 49152 | tf_op jit(solution)/shard_map/broadcast_in_dim | solution.py:471
  3.1 1.3 %broadcast_in_dim.27 = f32[2048]{0:T(1024)} convert(bf16[2048]{0:T(1024)(128)(2,1)} %param.15) | non-fusion elementwise | flops 2048 | bytes 12288 | tf_op jit(solution)/shard_map/broadcast_in_dim | solution.py:471
  4.4 74.4 %shard_map.127 = bf16[8,2048]{1,0:T(8,128)(2,1)} custom-call(s32[8]{0:T(128)} %slots_ref.1, s32[8]{0:T(128)} %lens_ref.1, bf16[32,8192]{1,0:T(8,128)(2,1)} %tok.1, f32[1,8192]{1,0:T(1,128)} %bitcast.2, f32[1,2048]{1,0:T(1,128)} %bitcast.3, f32[4,8,128]{2,1,0:T(8,128)} %get-tuple-element.8.cos, f32[4,8,128]{2,1,0:T(8,128)} %get-tuple-element.9.sin, ...), custom_call_target="tpu_custom_call" | custom-call | tf_op jit(solution)/shard_map/pallas_call | solution.py:461
  78.8 1.4 %copy.15 = bf16[8,2048]{1,0:T(8,128)(2,1)} copy(bf16[8,2048]{1,0:T(8,128)(2,1)} %shard_map.127) | data formatting | bytes 65536
  (2 shorter events, 0.0 us)
